TPU v7x, 256 devices: a whole 4x4x8 slice. The times are simulated.
256 devices in a mesh: row: 16 (over y, z_lo), col: 16 (over z_hi, x, core).
Axes of the slice: x: 4, y: 4, z: 8 (z_hi: 2, z_lo: 4; z = z_hi * 4 + z_lo), core: 2. Of those that a mesh axis runs over, the one named last changes fastest.
Arguments:
- laplacian: float32 [23040, 23040], P('row', 'col'), may hold values from -1 to 1.12, as said below
- block: float32 [23040, 256], P(('row', 'col')), may hold values from -6 to 6
- bounds: float32 [2], replicated, may hold values from 0.25 to 2.1, as said below
Outputs:
- filtered: float32 [23040, 256], P(('row', 'col'))
- rayleigh: float32 [256, 256], replicated
Inputs may be any that keep to these rules, and one draw needn't show every extreme that they name: laplacian is symmetric; its diagonal entries lie in 0.88 to 1.12 and its other entries have magnitude at most 1.14 / sqrt(23040). bounds[0] lies in 0.25 to 0.40 and bounds[1] in 1.95 to 2.10.
All inputs are finite; a program needn't handle non-finite values.
Results may differ from a plain program's by a relative error of at most 0.00025.
Values sent between devices are 32-bit elements; how exact they have to be, the bound alone decides.
A program may use at most 64 MiB of HBM per device.

v0:
```python
import jax
import jax.numpy as jnp
from jax import lax
from jax.sharding import PartitionSpec as P


def relayout(panel_rows, row_index, col_index, tile_rows, tile_cols):
    offset = col_index * tile_cols - row_index * tile_rows
    zeros_pad = jnp.zeros((tile_cols, panel_rows.shape[1]), jnp.float32)
    padded = jnp.concatenate([zeros_pad, panel_rows, zeros_pad], axis=0)
    start_row = jnp.clip(offset + tile_cols, 0, tile_rows + tile_cols)
    sliced = lax.dynamic_slice_in_dim(padded, start_row, tile_cols, 0)
    target = offset + lax.broadcasted_iota(jnp.int32, (tile_cols, 1), 0)
    inside = (target >= 0) & (target < tile_rows)
    return jnp.where(inside, sliced, 0.0)


def body(laplacian, block, bounds):
    row_index = lax.axis_index("row")
    col_index = lax.axis_index("col")
    tile_rows, tile_cols = laplacian.shape
    lower_bound = bounds[0]
    upper_bound = bounds[1]
    center = (upper_bound + lower_bound) * 0.5
    half_width = (upper_bound - lower_bound) * 0.5
    factor_two = 2.0 / half_width
    global_rows = row_index * tile_rows + lax.broadcasted_iota(jnp.int32, (tile_rows, tile_cols), 0)
    global_cols = col_index * tile_cols + lax.broadcasted_iota(jnp.int32, (tile_rows, tile_cols), 1)
    shifted = laplacian - center * (global_rows == global_cols).astype(jnp.float32)

    def through_columns(panel_rows):
        return lax.dot_general(
            shifted,
            panel_rows,
            (((0,), (0,)), ((), ())),
            precision=lax.Precision.HIGHEST,
            preferred_element_type=jnp.float32,
        )

    def through_rows(panel_cols):
        return jnp.dot(
            shifted, panel_cols, precision=lax.Precision.HIGHEST, preferred_element_type=jnp.float32
        )

    def gather_rows(values):
        return lax.all_gather(values, "col", axis=0, tiled=True)

    def gather_cols(values):
        return lax.all_gather(values, "row", axis=0, tiled=True)

    def column_sum(values):
        return lax.psum_scatter(values, "row", scatter_dimension=0, tiled=True)

    def row_sum(values):
        return lax.psum_scatter(values, "col", scatter_dimension=0, tiled=True)

    filter_one = column_sum(through_columns(gather_rows(block))) / half_width
    filter_two = factor_two * row_sum(through_rows(gather_cols(filter_one))) - block
    filter_three = factor_two * column_sum(through_columns(gather_rows(filter_two))) - filter_one
    filter_four = factor_two * row_sum(through_rows(gather_cols(filter_three))) - filter_two
    panel_four = gather_rows(filter_four)
    dims_inner = (((0,), (0,)), ((), ()))
    image_piece, moved_piece = (
        lax.psum_scatter(through_columns(panel_four), "row", scatter_dimension=0, tiled=True),
        lax.psum_scatter(
            relayout(panel_four, row_index, col_index, tile_rows, tile_cols),
            "row",
            scatter_dimension=0,
            tiled=True,
        ),
    )
    gram_part = lax.dot_general(
        moved_piece,
        moved_piece,
        dims_inner,
        precision=lax.Precision.HIGHEST,
        preferred_element_type=jnp.float32,
    )
    image_part = lax.dot_general(
        moved_piece,
        image_piece,
        dims_inner,
        precision=lax.Precision.HIGHEST,
        preferred_element_type=jnp.float32,
    )
    gram, projected = lax.psum((gram_part, image_part), ("row", "col"))
    projected = projected + center * gram
    projected = (projected + projected.T) * 0.5
    factor = jnp.linalg.cholesky(gram)
    first_solve = jax.scipy.linalg.solve_triangular(factor, projected, lower=True)
    rayleigh = jax.scipy.linalg.solve_triangular(factor, first_solve.T, lower=True)
    return (filter_four, rayleigh)


def solution(mesh):
    placed = (P("row", "col"), P(("row", "col"), None), P())
    return jax.shard_map(
        body, mesh=mesh, in_specs=placed, out_specs=(P(("row", "col"), None), P()), check_vma=False
    )
```

profile of v0, /device:TPU:2, one launch (start us, length us, event | category | flops | bytes accessed | tf_op | source)
XLA Modules:
  0.0 1090.3 jit_solution(2360731310481953332)
XLA Ops:
  7.2 0.7 all-gather.11.cloned.1.call-update
  8.0 1.3 fusion.44
  10.6 61.9 %all-gather.11.cloned.1.call-done = f32[16,90,256]{2,1,0:T(8,128)} async-done(((f32[1,90,256]{2,1,0:T(8,128)}), f32[16,90,256]{2,1,0:T(8,128)}) %all-gather.11.cloned.1.call-update) | async-done | bytes 1474576 | tf_op jit(solution)/shard_map/all_gather | solution.py:46
  72.5 1.5 reshape.61
  74.0 17.9 %fusion.41 = f32[1440,256]{1,0:T(8,128)S(1)} fusion(f32[1440,256]{1,0:T(8,128)S(1)} %reshape.61, f32[1440,1440]{1,0:T(8,128)} %param.5, f32[]{:T(128)} %bitcast.1, s32[1440]{0:T(1024)S(1)} %get-tuple-element.45, s32[1440]{0:T(1024)S(1)} %get-tuple-element.46), kind=kOutput, calls=%fused_computation.71 | convolution fusion | flops 6376320000 | bytes 11255044 | tf_op jit(solution)/shard_map/dot_general | solution.py:32
  91.8 55.3 %fusion = f32[96,256]{1,0:T(8,128)S(1)} fusion(f32[1440,256]{1,0:T(8,128)S(1)} %fusion.41), kind=kCustom, calls=%all-reduce-scatter | all-reduce-scatter fusion | flops 393217 | bytes 1573888
  147.1 1.3 collective-permute-start
  149.7 0.6 dynamic-slice.19
  151.3 0.7 fusion.30
  151.9 0.3 all-gather.15.cloned.1.call-start
  152.2 80.0 %all-gather.13.cloned.1.call-done = f32[16,90,256]{2,1,0:T(8,128)} async-done(((f32[1,90,256]{2,1,0:T(8,128)}), f32[16,90,256]{2,1,0:T(8,128)}) %all-gather.13.cloned.1.call-update) | async-done | bytes 1474576 | tf_op jit(solution)/shard_map/all_gather | solution.py:49
  232.3 1.5 reshape.63
  233.8 10.1 fusion.40
  243.9 48.1 %fusion.1 = f32[96,256]{1,0:T(8,128)S(1)} fusion(f32[1440,256]{1,0:T(8,128)S(1)} %fusion.40), kind=kCustom, calls=%all-reduce-scatter.1 | all-reduce-scatter fusion | flops 393217 | bytes 1573888
  292.0 1.9 collective-permute-start.1
  294.0 0.6 dynamic-slice.23
  295.2 2.7 collective-permute-done.1
  298.2 0.7 fusion.31
  298.9 66.9 %all-gather.15.cloned.1.call-done = f32[16,90,256]{2,1,0:T(8,128)} async-done(((f32[1,90,256]{2,1,0:T(8,128)}), f32[16,90,256]{2,1,0:T(8,128)}) %all-gather.15.cloned.1.call-update) | async-done | bytes 1474576 | tf_op jit(solution)/shard_map/all_gather | solution.py:46
  365.9 1.5 reshape.65
  367.4 17.9 %fusion.39 = f32[1440,256]{1,0:T(8,128)S(1)} fusion(f32[1440,256]{1,0:T(8,128)S(1)} %reshape.65, f32[1440,1440]{1,0:T(8,128)} %param.5, f32[]{:T(128)} %bitcast.1, s32[1440]{0:T(1024)S(1)} %get-tuple-element.45, s32[1440]{0:T(1024)S(1)} %get-tuple-element.46), kind=kOutput, calls=%fused_computation.69 | convolution fusion | flops 6376320000 | bytes 11255044 | tf_op jit(solution)/shard_map/dot_general | solution.py:32
  385.2 55.2 %fusion.2 = f32[96,256]{1,0:T(8,128)S(1)} fusion(f32[1440,256]{1,0:T(8,128)S(1)} %fusion.39), kind=kCustom, calls=%all-reduce-scatter.2 | all-reduce-scatter fusion | flops 393217 | bytes 1573888
  440.4 1.3 collective-permute-start.2
  441.7 2.2 collective-permute-done.2
  444.2 0.7 fusion.18
  444.9 10.4 all-gather.19.cloned.1.call-start
  455.3 70.4 %all-gather.17.cloned.1.call-done = f32[16,90,256]{2,1,0:T(8,128)} async-done(((f32[1,90,256]{2,1,0:T(8,128)}), f32[16,90,256]{2,1,0:T(8,128)}) %all-gather.17.cloned.1.call-update) | async-done | bytes 1474576 | tf_op jit(solution)/shard_map/all_gather | solution.py:49
  525.7 1.5 reshape.67
  527.1 10.1 fusion.38
  537.2 48.0 %fusion.3 = f32[96,256]{1,0:T(8,128)S(1)} fusion(f32[1440,256]{1,0:T(8,128)S(1)} %fusion.38), kind=kCustom, calls=%all-reduce-scatter.3 | all-reduce-scatter fusion | flops 393217 | bytes 1573888
  585.2 1.9 collective-permute-start.3
  587.2 4.0 collective-permute-done.3
  591.4 0.7 fusion.16
  592.2 66.9 %all-gather.19.cloned.1.call-done = f32[16,90,256]{2,1,0:T(8,128)} async-done(((f32[1,90,256]{2,1,0:T(8,128)}), f32[16,90,256]{2,1,0:T(8,128)}) %all-gather.19.cloned.1.call-update) | async-done | bytes 1474576 | tf_op jit(solution)/shard_map/all_gather | solution.py:46
  659.1 1.5 reshape.69
  660.6 19.0 %fusion.37 = f32[1440,256]{1,0:T(8,128)} fusion(f32[1440,256]{1,0:T(8,128)S(1)} %reshape.69, f32[1440,1440]{1,0:T(8,128)} %param.5, f32[]{:T(128)} %bitcast.1, s32[1440]{0:T(1024)S(1)} %get-tuple-element.45, s32[1440]{0:T(1024)S(1)} %get-tuple-element.46), kind=kOutput, calls=%fused_computation.67 | convolution fusion | flops 6376320000 | bytes 11255044 | tf_op jit(solution)/shard_map/dot_general | solution.py:32
  679.7 0.8 fusion.8
  680.5 74.2 %fusion.42 = (f32[96,256]{1,0:T(8,128)S(1)}, f32[96,256]{1,0:T(8,128)S(1)}) fusion(f32[1440,256]{1,0:T(8,128)} %fusion.37, f32[1440,256]{1,0:T(8,128)S(1)} %fusion.8), kind=kCustom, calls=%all-reduce-scatter.6 | all-reduce-scatter fusion | flops 786433 | bytes 3146752
  754.7 1.3 collective-permute-start.4
  756.0 1.5 collective-permute-start.5
  757.5 0.7 collective-permute-done.4
  758.4 1.1 fusion.21
  759.8 1.1 fusion.14
  761.0 256.2 %all-reduce.17.cloned.1.call-done = (f32[256,256]{0,1:T(8,128)}, f32[256,256]{0,1:T(8,128)}) async-done(((f32[256,256]{0,1:T(8,128)}, f32[256,256]{0,1:T(8,128)}), (f32[256,256]{0,1:T(8,128)}, f32[256,256]{0,1:T(8,128)})) %all-reduce.17.cloned.1.call-update) | async-done | bytes 524304 | tf_op jit(solution)/shard_map/psum | solution.py:86
  1017.2 1.1 copy.16
  1018.3 1.1 bitcast_add_fusion.1
  1019.6 11.7 %cholesky.50 = f32[128,128]{1,0:T(8,128)S(1)} custom-call(f32[128,128]{1,0:T(8,128)S(1)} %cholesky.118), custom_call_target="Cholesky" | custom-call | tf_op jit(solution)/shard_map/jit(cholesky)/cholesky | solution.py:89
  1031.4 9.8 custom-call.14
  1041.4 0.3 convolution_subtract_fusion.2
  1041.7 11.7 %cholesky.105 = f32[128,128]{1,0:T(8,128)S(1)} custom-call(f32[128,128]{1,0:T(8,128)S(1)} %convolution_subtract_fusion.2), custom_call_target="Cholesky" | custom-call | tf_op jit(solution)/shard_map/jit(cholesky)/cholesky | solution.py:89
  1053.4 0.7 compare_reduce_fusion
  1054.1 0.6 compare_reduce_fusion.1
  1056.2 4.1 while.4
  1056.2 0.6 fusion.57
  1056.8 1.4 bitcast_dynamic-update-slice_fusion.2
  1058.2 0.6 fusion.57
  1058.8 1.4 bitcast_dynamic-update-slice_fusion.2
  1060.3 19.9 %custom-call.17 = f32[2,128,128]{1,2,0:T(8,128)S(1)} custom-call(f32[2,128,128]{2,1,0:T(8,128)S(1)} %get-tuple-element.18), custom_call_target="InvertDiagBlocksLowerTriangular" | custom-call | tf_op jit(solution)/shard_map/jit(_solve_triangular)/triangular_solve | solution.py:91
  1080.4 0.3 fusion.12
  1080.9 0.3 fusion.27
  1081.3 0.3 fusion.10
  1081.6 0.4 convolution_subtract_fusion
  1082.0 0.3 fusion.26
  1082.3 0.7 pad_maximum_fusion
  (49 shorter events, 3.0 us)
Async XLA Ops:
  7.2 65.3 %all-gather.11.cloned.1.call-start = ((), (), s32[]{:S(2)}) async-start(), calls=%async_computation | async-start | bytes 1671168 | tf_op jit(solution)/shard_map/all_gather | solution.py:46
  7.9 224.4 %all-gather.13.cloned.1.call-start = ((), (), s32[]{:S(2)}) async-start(), calls=%async_computation.1 | async-start | bytes 1671168 | tf_op jit(solution)/shard_map/all_gather | solution.py:49
  91.8 57.9 %copy-start.2 = (u32[256]{0:T(256)S(1)}, u32[256]{0:T(256)}, u32[]{:S(2)}) copy-start(u32[256]{0:T(256)} %constant.130) | copy-start | bytes 3076
  147.1 3.9 collective-permute-start
  151.9 213.9 %all-gather.15.cloned.1.call-start = ((), (), s32[]{:S(2)}) async-start(), calls=%async_computation.2 | async-start | bytes 1671168 | tf_op jit(solution)/shard_map/all_gather | solution.py:46
  243.8 50.1 %copy-start.1 = (u32[256]{0:T(256)S(1)}, u32[256]{0:T(256)}, u32[]{:S(2)}) copy-start(u32[256]{0:T(256)} %constant.134) | copy-start | bytes 3076
  243.9 54.3 %copy-start = (f32[90,256]{1,0:T(8,128)S(1)}, f32[90,256]{1,0:T(8,128)}, u32[]{:S(2)}) copy-start(f32[90,256]{1,0:T(8,128)} %param.6) | copy-start | bytes 276484
  292.0 5.9 collective-permute-start.1
  298.9 226.8 %all-gather.17.cloned.1.call-start = ((), (), s32[]{:S(2)}) async-start(), calls=%async_computation.3 | async-start | bytes 1671168 | tf_op jit(solution)/shard_map/all_gather | solution.py:49
  440.4 3.5 collective-permute-start.2
  444.9 214.2 %all-gather.19.cloned.1.call-start = ((), (), s32[]{:S(2)}) async-start(), calls=%async_computation.4 | async-start | bytes 1671168 | tf_op jit(solution)/shard_map/all_gather | solution.py:46
  585.2 5.9 collective-permute-start.3
  592.1 425.1 %all-reduce.17.cloned.1.call-start = ((), (), s32[]{:S(2)}) async-start(), calls=%async_computation.5 | async-start | bytes 1048576 | tf_op jit(solution)/shard_map/psum | solution.py:86
  754.7 3.5 collective-permute-start.4
  756.0 3.6 collective-permute-start.5
Sparse Core Ops, SparseCore 0:
  10.7 61.7 all-gather.10
  152.1 80.1 all-gather.12
  299.0 66.7 all-gather.14
  445.0 80.5 all-gather.16
  592.3 66.7 all-gather.18
  761.1 256.0 all-reduce.16
where the time goes:
time: 1100 us; the launch traced here: 1090 us
  waiting for transfers between devices  613 us (56%)
  blocking collectives  281 us (26%)
  matrix products  79.5 us (7%)
  other arithmetic  60 us (5%)
  between operations  20.4 us (2%)
  starting transfers between devices  20.1 us (2%)
  local copies, waits for them, and re-layouts  17.1 us (2%)
    unnamed x5, blocking collectives  281 us
    psum x1, waiting for transfers between devices, body(): gram, projected = lax.psum((gram_part, image_part), ('row', 'col'))  256 us
    all_gather x3, waiting for transfers between devices, gather_rows(): return lax.all_gather(values, 'col', axis=0, tiled=True)  196 us
    all_gather x2, waiting for transfers between devices, gather_cols(): return lax.all_gather(values, 'row', axis=0, tiled=True)  150 us
    dot_general x3, matrix products, through_columns(): lax.dot_general(shifted, panel_rows, (((0,), (0,)), ((), ())), precision=...  54.7 us
    another operation x7, other arithmetic, body(): factor = jnp.linalg.cholesky(gram)  34.6 us
  transfers between devices with their start and end apart: 12, of which 10 were waited for; matrix products, arithmetic and copies ran while one was open for 0% of the time, Pallas kernels for 0%

commit v1 on v0

--- a/solution.py
+++ b/solution.py
@@ -83,7 +83,7 @@
         precision=lax.Precision.HIGHEST,
         preferred_element_type=jnp.float32,
     )
-    gram, projected = lax.psum((gram_part, image_part), ("row", "col"))
+    gram, projected = jax.lax.psum(jax.lax.psum((gram_part, image_part), "col"), "row")
     projected = projected + center * gram
     projected = (projected + projected.T) * 0.5
     factor = jnp.linalg.cholesky(gram)

time: 1100 us -> 1190 us (1.082)
  waiting for transfers between devices: 613 us -> 701 us
    psum x1 -> x2, waiting for transfers between devices: 256 us -> 345 us  [the longest x1 174 us: body(): jax.lax.psum(jax.lax.psum((gram_part, image_part), 'col'), 'row')]
  transfers between devices with their start and end apart: 12 -> 13, of which waited for: 10 -> 11; matrix products, arithmetic and copies ran while one was open for 0% -> 0% of each run, Pallas kernels for 0% -> 0%
where the time goes in v1:
time: 1190 us; the launch traced here: 1180 us
  waiting for transfers between devices  701 us (59%)
  blocking collectives  281 us (24%)
  matrix products  79.5 us (7%)
  other arithmetic  59.7 us (5%)
  starting transfers between devices  20.7 us (2%)
  between operations  20.3 us (2%)
  local copies, waits for them, and re-layouts  17 us (1%)
    unnamed x5, blocking collectives  281 us
    all_gather x3, waiting for transfers between devices, gather_rows(): return lax.all_gather(values, 'col', axis=0, tiled=True)  196 us
    psum x1, waiting for transfers between devices, body(): jax.lax.psum(jax.lax.psum((gram_part, image_part), 'col'), 'row')  174 us
    psum x1, waiting for transfers between devices, body(): jax.lax.psum((gram_part, image_part), 'col')  171 us
    all_gather x2, waiting for transfers between devices, gather_cols(): return lax.all_gather(values, 'row', axis=0, tiled=True)  150 us
    dot_general x3, matrix products, through_columns(): lax.dot_general(shifted, panel_rows, (((0,), (0,)), ((), ())), precision=...  54.7 us
    another operation x7, other arithmetic, body(): factor = jnp.linalg.cholesky(gram)  34.6 us
  transfers between devices with their start and end apart: 13, of which 11 were waited for; matrix products, arithmetic and copies ran while one was open for 0% of the time, Pallas kernels for 0%

profile of v1, /device:TPU:2, one launch (start us, length us, event | category | flops | bytes accessed | tf_op | source)
XLA Modules:
  0.0 1179.3 jit_solution(10831064368036775651)
XLA Ops:
  7.2 0.7 all-gather.11.cloned.1.call-update
  8.0 1.3 fusion.44
  10.6 61.9 %all-gather.11.cloned.1.call-done = f32[16,90,256]{2,1,0:T(8,128)} async-done(((f32[1,90,256]{2,1,0:T(8,128)}), f32[16,90,256]{2,1,0:T(8,128)}) %all-gather.11.cloned.1.call-update) | async-done | bytes 1474576 | tf_op jit(solution)/shard_map/all_gather | solution.py:46
  72.5 1.5 reshape.61
  74.0 17.9 %fusion.41 = f32[1440,256]{1,0:T(8,128)S(1)} fusion(f32[1440,256]{1,0:T(8,128)S(1)} %reshape.61, f32[1440,1440]{1,0:T(8,128)} %param.5, f32[]{:T(128)} %bitcast.1, s32[1440]{0:T(1024)S(1)} %get-tuple-element.47, s32[1440]{0:T(1024)S(1)} %get-tuple-element.48), kind=kOutput, calls=%fused_computation.71 | convolution fusion | flops 6376320000 | bytes 11255044 | tf_op jit(solution)/shard_map/dot_general | solution.py:32
  91.8 55.3 %fusion = f32[96,256]{1,0:T(8,128)S(1)} fusion(f32[1440,256]{1,0:T(8,128)S(1)} %fusion.41), kind=kCustom, calls=%all-reduce-scatter | all-reduce-scatter fusion | flops 393217 | bytes 1573888
  147.1 1.3 collective-permute-start
  149.7 0.6 dynamic-slice.19
  151.3 0.7 fusion.30
  151.9 0.3 all-gather.15.cloned.1.call-start
  152.2 80.0 %all-gather.13.cloned.1.call-done = f32[16,90,256]{2,1,0:T(8,128)} async-done(((f32[1,90,256]{2,1,0:T(8,128)}), f32[16,90,256]{2,1,0:T(8,128)}) %all-gather.13.cloned.1.call-update) | async-done | bytes 1474576 | tf_op jit(solution)/shard_map/all_gather | solution.py:49
  232.3 1.5 reshape.63
  233.8 10.1 fusion.40
  243.9 48.1 %fusion.1 = f32[96,256]{1,0:T(8,128)S(1)} fusion(f32[1440,256]{1,0:T(8,128)S(1)} %fusion.40), kind=kCustom, calls=%all-reduce-scatter.1 | all-reduce-scatter fusion | flops 393217 | bytes 1573888
  292.0 1.9 collective-permute-start.1
  294.0 0.6 dynamic-slice.23
  295.2 2.7 collective-permute-done.1
  298.2 0.7 fusion.31
  298.9 66.9 %all-gather.15.cloned.1.call-done = f32[16,90,256]{2,1,0:T(8,128)} async-done(((f32[1,90,256]{2,1,0:T(8,128)}), f32[16,90,256]{2,1,0:T(8,128)}) %all-gather.15.cloned.1.call-update) | async-done | bytes 1474576 | tf_op jit(solution)/shard_map/all_gather | solution.py:46
  365.9 1.5 reshape.65
  367.4 17.9 %fusion.39 = f32[1440,256]{1,0:T(8,128)S(1)} fusion(f32[1440,256]{1,0:T(8,128)S(1)} %reshape.65, f32[1440,1440]{1,0:T(8,128)} %param.5, f32[]{:T(128)} %bitcast.1, s32[1440]{0:T(1024)S(1)} %get-tuple-element.47, s32[1440]{0:T(1024)S(1)} %get-tuple-element.48), kind=kOutput, calls=%fused_computation.69 | convolution fusion | flops 6376320000 | bytes 11255044 | tf_op jit(solution)/shard_map/dot_general | solution.py:32
  385.2 55.2 %fusion.2 = f32[96,256]{1,0:T(8,128)S(1)} fusion(f32[1440,256]{1,0:T(8,128)S(1)} %fusion.39), kind=kCustom, calls=%all-reduce-scatter.2 | all-reduce-scatter fusion | flops 393217 | bytes 1573888
  440.4 1.3 collective-permute-start.2
  441.7 2.2 collective-permute-done.2
  444.2 0.7 fusion.18
  444.9 11.0 all-gather.19.cloned.1.call-start
  455.9 69.8 %all-gather.17.cloned.1.call-done = f32[16,90,256]{2,1,0:T(8,128)} async-done(((f32[1,90,256]{2,1,0:T(8,128)}), f32[16,90,256]{2,1,0:T(8,128)}) %all-gather.17.cloned.1.call-update) | async-done | bytes 1474576 | tf_op jit(solution)/shard_map/all_gather | solution.py:49
  525.7 1.5 reshape.67
  527.1 10.1 fusion.38
  537.2 47.9 %fusion.3 = f32[96,256]{1,0:T(8,128)S(1)} fusion(f32[1440,256]{1,0:T(8,128)S(1)} %fusion.38), kind=kCustom, calls=%all-reduce-scatter.3 | all-reduce-scatter fusion | flops 393217 | bytes 1573888
  585.2 1.9 collective-permute-start.3
  587.1 4.0 collective-permute-done.3
  591.4 0.7 fusion.16
  592.2 66.8 %all-gather.19.cloned.1.call-done = f32[16,90,256]{2,1,0:T(8,128)} async-done(((f32[1,90,256]{2,1,0:T(8,128)}), f32[16,90,256]{2,1,0:T(8,128)}) %all-gather.19.cloned.1.call-update) | async-done | bytes 1474576 | tf_op jit(solution)/shard_map/all_gather | solution.py:46
  659.0 1.5 reshape.69
  660.5 19.0 %fusion.37 = f32[1440,256]{1,0:T(8,128)} fusion(f32[1440,256]{1,0:T(8,128)S(1)} %reshape.69, f32[1440,1440]{1,0:T(8,128)} %param.5, f32[]{:T(128)} %bitcast.1, s32[1440]{0:T(1024)S(1)} %get-tuple-element.47, s32[1440]{0:T(1024)S(1)} %get-tuple-element.48), kind=kOutput, calls=%fused_computation.67 | convolution fusion | flops 6376320000 | bytes 11255044 | tf_op jit(solution)/shard_map/dot_general | solution.py:32
  679.6 0.8 fusion.8
  680.4 74.2 %fusion.42 = (f32[96,256]{1,0:T(8,128)S(1)}, f32[96,256]{1,0:T(8,128)S(1)}) fusion(f32[1440,256]{1,0:T(8,128)} %fusion.37, f32[1440,256]{1,0:T(8,128)S(1)} %fusion.8), kind=kCustom, calls=%all-reduce-scatter.6 | all-reduce-scatter fusion | flops 786433 | bytes 3146752
  754.6 1.3 collective-permute-start.4
  755.9 1.3 collective-permute-start.5
  757.2 0.9 collective-permute-done.4
  758.4 1.1 fusion.21
  759.7 1.1 fusion.14
  761.2 171.4 %all-reduce.19.cloned.1.call-done = (f32[256,256]{0,1:T(8,128)}, f32[256,256]{0,1:T(8,128)}) async-done(((f32[256,256]{0,1:T(8,128)}, f32[256,256]{0,1:T(8,128)}), (f32[256,256]{0,1:T(8,128)}, f32[256,256]{0,1:T(8,128)})) %all-reduce.19.cloned.1.call-update) | async-done | bytes 524304 | tf_op jit(solution)/shard_map/psum | solution.py:86
  932.6 173.8 %all-reduce.21.cloned.1.call-done = (f32[256,256]{0,1:T(8,128)}, f32[256,256]{0,1:T(8,128)}) async-done(((f32[256,256]{0,1:T(8,128)}, f32[256,256]{0,1:T(8,128)}), (f32[256,256]{0,1:T(8,128)}, f32[256,256]{0,1:T(8,128)})) %all-reduce.21.cloned.1.call-update) | async-done | bytes 524304 | tf_op jit(solution)/shard_map/psum | solution.py:86
  1106.4 1.1 copy.16
  1107.4 1.1 bitcast_add_fusion.1
  1108.7 11.7 cholesky.50
  1120.5 9.8 custom-call.14
  1130.8 11.7 cholesky.105
  1142.5 0.7 compare_reduce_fusion
  1143.2 0.6 compare_reduce_fusion.1
  1145.2 4.2 while.4
  1145.5 0.6 fusion.57
  1146.1 1.4 bitcast_dynamic-update-slice_fusion.2
  1147.5 0.6 fusion.57
  1148.0 1.4 bitcast_dynamic-update-slice_fusion.2
  1149.4 19.7 %custom-call.17 = f32[2,128,128]{1,2,0:T(8,128)S(1)} custom-call(f32[2,128,128]{2,1,0:T(8,128)S(1)} %get-tuple-element.18), custom_call_target="InvertDiagBlocksLowerTriangular" | custom-call | tf_op jit(solution)/shard_map/jit(_solve_triangular)/triangular_solve | solution.py:91
  1169.3 0.3 fusion.12
  1169.9 0.3 fusion.27
  1170.2 0.3 fusion.10
  1170.5 0.4 convolution_subtract_fusion
  1170.9 0.3 fusion.26
  1171.3 0.7 pad_maximum_fusion
  (52 shorter events, 3.5 us)
Async XLA Ops:
  7.2 65.3 %all-gather.11.cloned.1.call-start = ((), (), s32[]{:S(2)}) async-start(), calls=%async_computation | async-start | bytes 1671168 | tf_op jit(solution)/shard_map/all_gather | solution.py:46
  7.9 224.4 %all-gather.13.cloned.1.call-start = ((), (), s32[]{:S(2)}) async-start(), calls=%async_computation.1 | async-start | bytes 1671168 | tf_op jit(solution)/shard_map/all_gather | solution.py:49
  91.8 57.9 %copy-start.2 = (u32[256]{0:T(256)S(1)}, u32[256]{0:T(256)}, u32[]{:S(2)}) copy-start(u32[256]{0:T(256)} %constant.130) | copy-start | bytes 3076
  147.1 3.9 collective-permute-start
  151.9 213.9 %all-gather.15.cloned.1.call-start = ((), (), s32[]{:S(2)}) async-start(), calls=%async_computation.2 | async-start | bytes 1671168 | tf_op jit(solution)/shard_map/all_gather | solution.py:46
  243.8 50.1 %copy-start.1 = (u32[256]{0:T(256)S(1)}, u32[256]{0:T(256)}, u32[]{:S(2)}) copy-start(u32[256]{0:T(256)} %constant.134) | copy-start | bytes 3076
  243.9 54.3 %copy-start = (f32[90,256]{1,0:T(8,128)S(1)}, f32[90,256]{1,0:T(8,128)}, u32[]{:S(2)}) copy-start(f32[90,256]{1,0:T(8,128)} %param.6) | copy-start | bytes 276484
  292.0 5.9 collective-permute-start.1
  298.9 226.8 %all-gather.17.cloned.1.call-start = ((), (), s32[]{:S(2)}) async-start(), calls=%async_computation.3 | async-start | bytes 1671168 | tf_op jit(solution)/shard_map/all_gather | solution.py:49
  440.4 3.5 collective-permute-start.2
  444.9 214.1 %all-gather.19.cloned.1.call-start = ((), (), s32[]{:S(2)}) async-start(), calls=%async_computation.4 | async-start | bytes 1671168 | tf_op jit(solution)/shard_map/all_gather | solution.py:46
  585.2 5.9 collective-permute-start.3
  592.1 340.4 %all-reduce.19.cloned.1.call-start = ((), (), s32[]{:S(2)}) async-start(), calls=%async_computation.5 | async-start | bytes 1048576 | tf_op jit(solution)/shard_map/psum | solution.py:86
  754.6 3.5 collective-permute-start.4
  755.9 3.6 collective-permute-start.5
  760.9 345.5 %all-reduce.21.cloned.1.call-start = ((), (), s32[]{:S(2)}) async-start(), calls=%async_computation.6 | async-start | bytes 1048576 | tf_op jit(solution)/shard_map/psum | solution.py:86
Sparse Core Ops, SparseCore 0:
  10.7 61.7 all-gather.10
  152.1 80.1 all-gather.12
  299.0 66.7 all-gather.14
  445.0 80.5 all-gather.16
  592.2 66.7 all-gather.18
  761.0 171.4 all-reduce.18
  935.2 171.1 all-reduce.20
